TPU v7x, 512 devices: a whole 4x8x8 slice. The times are simulated.
512 devices in a mesh: pages: 64 (over y, z_lo, core), heads: 8 (over x, z_hi).
Axes of the slice: x: 4, y: 8, z: 8 (z_hi: 2, z_lo: 4; z = z_hi * 4 + z_lo), core: 2. Of those that a mesh axis runs over, the one named last changes fastest.
Arguments:
- candidates: bfloat16 [49152, 1024], P(('pages', 'heads')), may hold values from -6 to 6
- in_weight: bfloat16 [2, 1024, 8, 512], P(None, None, 'heads'), may hold values from -0.1875 to 0.1875
- out_weight: bfloat16 [2, 8, 128, 1024], P(None, 'heads'), may hold values from -0.1875 to 0.1875
- page_cache: bfloat16 [2, 4096, 8, 2, 32, 128], P(None, 'pages', 'heads'), may hold values from -6 to 6
- page_lists: int32 [1024, 4], P('pages'), may hold values from 0 to 4095, as said below
- hist_len: int32 [1024], P('pages'), may hold values from 1 to 128
Outputs:
- hidden_out: bfloat16 [49152, 1024], P(('pages', 'heads'))
Inputs may be any that keep to these rules, and one draw needn't show every extreme that they name: `page_lists`: every page id appears in exactly one list. Page p lies on index p // 64 of pages; the requests of one index of pages list either none or exactly 2 pages that lie on any one index.
All inputs are finite; a program needn't handle non-finite values.
Results may differ from a plain program's by a relative error of at most 0.018.
Values may be sent and summed in bfloat16 or wider, within the bound.
A program may use at most 64 MiB of HBM per device.

v0:
```python
import math
import jax
import jax.numpy as jnp
from jax import lax
from jax.sharding import PartitionSpec as P

eps = 1e-05


def layer_norm(values):
    row_mean = jnp.mean(values, -1, keepdims=True)
    centred = values - row_mean
    spread = jnp.mean(centred * centred, -1, keepdims=True)
    return centred * lax.rsqrt(spread + eps)


def gather_rows(rows):
    return lax.all_gather(rows, "heads", axis=0, tiled=True)


def scatter_sum(terms):
    return lax.psum_scatter(terms, "heads", scatter_dimension=0, tiled=True).astype(jnp.float32)


def on_device(candidates, in_weight, out_weight, page_cache, page_lists, hist_len):
    readers = lax.axis_size("pages")
    head_group = lax.axis_size("heads")
    layers = in_weight.shape[0]
    model_width = in_weight.shape[1]
    head_dim = out_weight.shape[2]
    pages_here = page_cache.shape[1]
    page_len = page_cache.shape[4]
    requests, max_pages = page_lists.shape
    slot_count = requests * max_pages
    capacity = 2 * slot_count // readers
    cand_rows = candidates.shape[0] * head_group
    per_request = cand_rows // requests
    history = max_pages * page_len
    score_scale = 1.0 / math.sqrt(head_dim)
    flat_ids = page_lists.reshape(slot_count)
    slot_owner = flat_ids // pages_here
    local_ids = flat_ids % pages_here
    slot_order = jnp.arange(slot_count)
    earlier_same = (slot_owner[None, :] == slot_owner[:, None]) & (
        slot_order[None, :] < slot_order[:, None]
    )
    slot_rank = jnp.sum(earlier_same.astype(jnp.int32), axis=1)
    places = slot_owner * capacity + slot_rank
    matches = places[None, :] == jnp.arange(readers * capacity)[:, None]
    asked = jnp.sum(jnp.where(matches, local_ids[None, :], 0), axis=1)
    wanted = lax.all_to_all(
        asked.reshape(readers, capacity), "pages", split_axis=0, concat_axis=0, tiled=True
    ).reshape(readers * capacity)
    histories = []
    for layer_index in range(layers):
        sent = jnp.take(page_cache[layer_index, :, 0], wanted, axis=0)
        if histories:
            sent, histories[-1] = lax.optimization_barrier((sent, histories[-1]))
        histories.append(
            lax.all_to_all(
                sent.reshape((readers, capacity) + sent.shape[1:]),
                "pages",
                split_axis=0,
                concat_axis=0,
                tiled=True,
            )
        )
    divisors = (hist_len + 1).astype(jnp.float32)
    cand_divisors = jnp.repeat(divisors, per_request)
    live = jnp.arange(history)[None, :] < hist_len[:, None]
    hidden_rows = candidates
    for layer_index in range(layers):
        weights_in = in_weight[layer_index].reshape(model_width, 4 * head_dim)
        ready = layer_norm(gather_rows(hidden_rows).astype(jnp.float32)).astype(jnp.bfloat16)
        projected = jax.nn.silu(jnp.dot(ready, weights_in, preferred_element_type=jnp.float32))
        gate_part = projected[:, :head_dim]
        value_part = projected[:, head_dim : 2 * head_dim].astype(jnp.bfloat16)
        query_part = projected[:, 2 * head_dim : 3 * head_dim].astype(jnp.bfloat16)
        key_part = projected[:, 3 * head_dim :].astype(jnp.bfloat16)
        got, query_part = lax.optimization_barrier((histories[layer_index], query_part))
        got = got.reshape(readers * capacity, 2, page_len, head_dim)
        listed = jnp.take(got, places, axis=0).reshape(requests, max_pages, 2, page_len, head_dim)
        hist_keys = listed[:, :, 0].reshape(requests, history, head_dim)
        hist_values = listed[:, :, 1].reshape(requests, history, head_dim)
        queries = query_part.reshape(requests, per_request, head_dim)
        scores = (
            jnp.einsum("rqd,rtd->rqt", queries, hist_keys, preferred_element_type=jnp.float32)
            * score_scale
        )
        weights = (
            jnp.where(live[:, None, :], jax.nn.silu(scores), 0.0) / divisors[:, None, None]
        ).astype(jnp.bfloat16)
        attended = jnp.einsum(
            "rqt,rtd->rqd", weights, hist_values, preferred_element_type=jnp.float32
        ).reshape(cand_rows, head_dim)
        self_score = (
            jnp.sum(query_part.astype(jnp.float32) * key_part.astype(jnp.float32), -1) * score_scale
        )
        self_weight = (jax.nn.silu(self_score) / cand_divisors).astype(jnp.bfloat16)
        attended = attended + self_weight.astype(jnp.float32)[:, None] * value_part.astype(
            jnp.float32
        )
        gated_rows = (layer_norm(attended) * gate_part).astype(jnp.bfloat16)
        weights_out = out_weight[layer_index].reshape(head_dim, model_width)
        terms = jnp.dot(gated_rows, weights_out, preferred_element_type=jnp.float32)
        summed = scatter_sum(terms.astype(jnp.bfloat16))
        hidden_rows = (hidden_rows.astype(jnp.float32) + summed).astype(jnp.bfloat16)
    return hidden_rows


def solution(mesh):
    in_specs = (
        P(("pages", "heads"), None),
        P(None, None, "heads", None),
        P(None, "heads", None, None),
        P(None, "pages", "heads", None, None, None),
        P("pages", None),
        P("pages"),
    )
    out_specs = P(("pages", "heads"), None)
    return jax.shard_map(
        on_device, mesh=mesh, in_specs=in_specs, out_specs=out_specs, check_vma=False
    )
```

profile of v0, /device:TPU:8, one launch (start us, length us, event | category | flops | bytes accessed | tf_op | source)
XLA Modules:
  0.0 485.0 jit_solution(15698231655504196997)
XLA Ops:
  6.5 0.8 copy.31
  7.4 0.2 convert_reduce_fusion.2
  7.6 0.1 select_reduce_fusion
  7.7 0.8 all_to_all.12
  8.5 13.5 %all-to-all-start = ((s32[64,1,2]{2,1,0:T(1,128)}), s32[64,1,2]{2,1,0:T(1,128)S(1)}, u32[]{:S(2)}, u32[]{:S(2)}) async-start(s32[64,1,2]{2,1,0:T(1,128)} %bitcast), calls=%async_computation | async-start | bytes 65536 | tf_op jit(solution)/shard_map/all_to_all | solution.py:51
  22.0 2.0 slice_bitcast_fusion
  24.0 6.8 %all-to-all-done = s32[64,1,2]{2,1,0:T(1,128)S(1)} async-done(((s32[64,1,2]{2,1,0:T(1,128)}), s32[64,1,2]{2,1,0:T(1,128)S(1)}, u32[]{:S(2)}, u32[]{:S(2)}) %all-to-all-start) | async-done | bytes 544 | tf_op jit(solution)/shard_map/all_to_all | solution.py:51
  30.8 0.5 broadcast.307
  31.3 0.7 reduce.3
  32.0 0.1 reshape.241
  32.2 2.2 gather_fusion
  34.4 2.1 gather_fusion.1
  36.5 4.0 broadcast_select_fusion
  40.5 5.8 %all-to-all-start.1 = ((bf16[64,2,2,32,128]{4,3,2,1,0:T(8,128)(2,1)}), bf16[64,2,2,32,128]{4,3,2,1,0:T(8,128)(2,1)S(1)}, u32[]{:S(2)}, u32[]{:S(2)}) async-start(bf16[64,2,2,32,128]{4,3,2,1,0:T(8,128)(2,1)} %bitcast.3), calls=%async_computation.1 | async-start | bytes 4194304 | tf_op jit(solution)/shard_map/all_to_all | solution.py:60
  46.3 0.7 all-gather.3.cloned.1.call-update
  47.3 104.0 %all-gather.3.cloned.1.call-done = bf16[768,1024]{1,0:T(8,128)(2,1)} async-done(((bf16[96,1024]{1,0:T(8,128)(2,1)}), bf16[768,1024]{1,0:T(8,128)(2,1)}) %all-gather.3.cloned.1.call-update) | async-done | bytes 1572880 | tf_op jit(solution)/shard_map/all_gather | solution.py:18
  151.3 1.8 convert_reduce_fusion.1
  153.2 0.6 fusion.6
  153.8 3.9 fusion.65
  157.7 0.2 copy.33
  157.9 0.6 copy-done.6
  158.5 0.7 gather_fusion.2
  159.3 0.2 broadcast_select_fusion.3
  159.5 0.1 fusion.64
  159.6 0.6 fusion.31
  160.2 0.2 copy.36
  160.4 0.3 copy-done.7
  160.8 0.1 multiply_reduce_fusion.2
  160.9 2.8 convolution_convert_fusion.1
  163.7 8.5 %all-to-all-start.2 = ((bf16[64,2,2,32,128]{4,3,2,1,0:T(8,128)(2,1)}), bf16[64,2,2,32,128]{4,3,2,1,0:T(8,128)(2,1)S(1)}, u32[]{:S(2)}, u32[]{:S(2)}) async-start(bf16[64,2,2,32,128]{4,3,2,1,0:T(8,128)(2,1)} %bitcast.12), calls=%async_computation.3 | async-start | bytes 4194304 | tf_op jit(solution)/shard_map/all_to_all | solution.py:60
  172.2 124.9 %reduce-scatter.3.cloned.1.call-done = bf16[96,1024]{1,0:T(8,128)(2,1)} async-done(((bf16[768,1024]{1,0:T(8,128)(2,1)}), bf16[96,1024]{1,0:T(8,128)(2,1)}) %reduce-scatter.3.cloned.1.call-update) | async-done | bytes 196624 | tf_op jit(solution)/shard_map/reduce_scatter | solution.py:22
  297.1 1.7 add_convert_fusion.1
  298.8 0.2 reduce-scatter.5.cloned.1.call-start
  299.0 71.7 %all-gather.5.cloned.1.call-done = bf16[768,1024]{1,0:T(8,128)(2,1)} async-done(((bf16[96,1024]{1,0:T(8,128)(2,1)}), bf16[768,1024]{1,0:T(8,128)(2,1)}) %all-gather.5.cloned.1.call-update) | async-done | bytes 1572880 | tf_op jit(solution)/shard_map/all_gather | solution.py:18
  370.7 1.8 convert_reduce_fusion
  372.6 0.6 fusion.4
  373.2 3.9 fusion.66
  377.1 0.2 copy.37
  377.3 0.6 copy-done.4
  377.9 0.7 gather_fusion.3
  378.7 0.2 broadcast_select_fusion.2
  378.8 0.1 fusion.63
  379.0 0.6 fusion.30
  379.6 0.2 copy.40
  379.8 0.3 copy-done.5
  380.3 2.8 convolution_convert_fusion
  383.1 93.7 %reduce-scatter.5.cloned.1.call-done = bf16[96,1024]{1,0:T(8,128)(2,1)} async-done(((bf16[768,1024]{1,0:T(8,128)(2,1)}), bf16[96,1024]{1,0:T(8,128)(2,1)}) %reduce-scatter.5.cloned.1.call-update) | async-done | bytes 196624 | tf_op jit(solution)/shard_map/reduce_scatter | solution.py:22
  476.8 1.7 add_convert_fusion
  (57 shorter events, 1.2 us)
Async XLA Ops:
  8.5 22.3 %all-to-all-start = ((s32[64,1,2]{2,1,0:T(1,128)}), s32[64,1,2]{2,1,0:T(1,128)S(1)}, u32[]{:S(2)}, u32[]{:S(2)}) async-start(s32[64,1,2]{2,1,0:T(1,128)} %bitcast), calls=%async_computation | async-start | bytes 65536 | tf_op jit(solution)/shard_map/all_to_all | solution.py:51
  34.4 2.1 copy-start
  40.5 6.5 %copy-start.11 = (s32[16]{0:T(128)S(1)}, s32[16]{0:T(128)}, u32[]{:S(2)}) copy-start(s32[16]{0:T(128)} %param.15) | copy-start | bytes 196
  40.5 117.2 %all-to-all-start.1 = ((bf16[64,2,2,32,128]{4,3,2,1,0:T(8,128)(2,1)}), bf16[64,2,2,32,128]{4,3,2,1,0:T(8,128)(2,1)S(1)}, u32[]{:S(2)}, u32[]{:S(2)}) async-start(bf16[64,2,2,32,128]{4,3,2,1,0:T(8,128)(2,1)} %bitcast.3), calls=%async_computation.1 | async-start | bytes 4194304 | tf_op jit(solution)/shard_map/all_to_all | solution.py:60
  46.3 105.0 %all-gather.3.cloned.1.call-start = ((), (), s32[]{:S(2)}) async-start(), calls=%async_computation.5 | async-start | bytes 1769472 | tf_op jit(solution)/shard_map/all_gather | solution.py:18
  47.0 250.1 %reduce-scatter.3.cloned.1.call-start = ((), (), s32[]{:S(2)}) async-start(), calls=%async_computation.6 | async-start | bytes 1769472 | tf_op jit(solution)/shard_map/reduce_scatter | solution.py:22
  151.3 1.9 copy-start.1
  157.7 0.9 copy-start.6
  159.6 1.1 copy-start.7
  159.6 1.3 copy-start.9
  163.7 133.4 %copy-start.8 = (bf16[96,1024]{1,0:T(8,128)(2,1)S(1)}, bf16[96,1024]{1,0:T(8,128)(2,1)}, u32[]{:S(2)}) copy-start(bf16[96,1024]{1,0:T(8,128)(2,1)} %param.10) | copy-start | bytes 589828
  163.7 213.3 %all-to-all-start.2 = ((bf16[64,2,2,32,128]{4,3,2,1,0:T(8,128)(2,1)}), bf16[64,2,2,32,128]{4,3,2,1,0:T(8,128)(2,1)S(1)}, u32[]{:S(2)}, u32[]{:S(2)}) async-start(bf16[64,2,2,32,128]{4,3,2,1,0:T(8,128)(2,1)} %bitcast.12), calls=%async_computation.3 | async-start | bytes 4194304 | tf_op jit(solution)/shard_map/all_to_all | solution.py:60
  172.2 198.5 %all-gather.5.cloned.1.call-start = ((), (), s32[]{:S(2)}) async-start(), calls=%async_computation.7 | async-start | bytes 1769472 | tf_op jit(solution)/shard_map/all_gather | solution.py:18
  298.8 178.0 %reduce-scatter.5.cloned.1.call-start = ((), (), s32[]{:S(2)}) async-start(), calls=%async_computation.8 | async-start | bytes 1769472 | tf_op jit(solution)/shard_map/reduce_scatter | solution.py:22
  370.7 1.9 copy-start.2
  377.0 0.9 copy-start.4
  378.9 1.1 copy-start.5
  379.0 1.3 copy-start.10
  380.3 96.5 %copy-start.3 = (bf16[96,1024]{1,0:T(8,128)(2,1)S(1)}, bf16[96,1024]{1,0:T(8,128)(2,1)}, u32[]{:S(2)}) copy-start(bf16[96,1024]{1,0:T(8,128)(2,1)} %add_convert_fusion.1) | copy-start | bytes 589828
Sparse Core Ops, SparseCore 0:
  50.3 101.0 all-gather.2
  163.8 133.2 reduce-scatter.2
  300.3 70.3 all-gather.4
  383.2 93.4 reduce-scatter.4
where the time goes:
time: 486 us; the launch traced here: 485 us
  waiting for transfers between devices  402 us (83%)
  starting transfers between devices  28.1 us (6%)
  matrix products  14.5 us (3%)
  other arithmetic  14 us (3%)
  between operations  13.5 us (3%)
  local copies, waits for them, and re-layouts  13.1 us (3%)
    reduce_scatter x2, waiting for transfers between devices, scatter_sum(): lax.psum_scatter(terms, 'heads', scatter_dimension=0, tiled=True)  219 us
    all_gather x2, waiting for transfers between devices, gather_rows(): return lax.all_gather(rows, 'heads', axis=0, tiled=True)  176 us
    all_to_all x2, starting transfers between devices, on_device(): lax.all_to_all(sent.reshape((readers, capacity) + sent.shape[1:]), 'pages...  14.2 us
    all_to_all x1, starting transfers between devices, on_device(): lax.all_to_all(asked.reshape(readers, capacity), 'pages', split_axis=0, c...  13.5 us
  transfers between devices with their start and end apart: 7, of which 5 were waited for; matrix products, arithmetic and copies ran while one was open for 3% of the time, Pallas kernels for 0%

commit v1 on v0

--- a/solution.py
+++ b/solution.py
@@ -15,7 +15,9 @@
 
 
 def gather_rows(rows):
-    return lax.all_gather(rows, "heads", axis=0, tiled=True)
+    return jnp.concatenate(
+        lax.all_to_all(jnp.stack([rows] * lax.axis_size("heads")), "heads", 0, 0), axis=0
+    )
 
 
 def scatter_sum(terms):

time: 486 us -> 447 us (0.920)
  waiting for transfers between devices: 402 us -> 293 us
  blocking collectives: 0 us -> 49 us
  starting transfers between devices: 28.1 us -> 48.1 us
  local copies, waits for them, and re-layouts: 13.1 us -> 19.4 us
    all_gather x2 -> x0, waiting for transfers between devices: 176 us -> none  [gather_rows(): return lax.all_gather(rows, 'heads', axis=0, tiled=True)]
    all_to_all x2, waiting for transfers between devices: 0.01 us -> 91.4 us  [on_device(): lax.all_to_all(sent.reshape((readers, capacity) + sent.shape[1:]), 'pages...]
    all_to_all x0 -> x2, blocking collectives: none -> 49 us  [the longest x1 26.8 us: gather_rows(): lax.all_to_all(jnp.stack([rows] * lax.axis_size('heads')), 'heads', 0, 0)]
    reduce_scatter x2, waiting for transfers between devices: 219 us -> 181 us  [scatter_sum(): lax.psum_scatter(terms, 'heads', scatter_dimension=0, tiled=True)]
    all_to_all x2, starting transfers between devices: 14.2 us -> 37.8 us  [on_device(): lax.all_to_all(sent.reshape((readers, capacity) + sent.shape[1:]), 'pages...]
    all_to_all x1, waiting for transfers between devices: 6.83 us -> 20.7 us  [gather_rows(): lax.all_to_all(jnp.stack([rows] * lax.axis_size('heads')), 'heads', 0, 0)]
  transfers between devices with their start and end apart: 7 -> 5, of which waited for: 5 -> 5; matrix products, arithmetic and copies ran while one was open for 3% -> 5% of each run, Pallas kernels for 0% -> 0%
where the time goes in v1:
time: 447 us
  waiting for transfers between devices  293 us (66%)
  blocking collectives  49 us (11%)
  starting transfers between devices  48.1 us (11%)
  local copies, waits for them, and re-layouts  19.4 us (4%)
  between operations  13.8 us (3%)
  other arithmetic  11.8 us (3%)
  matrix products  11.6 us (3%)
    reduce_scatter x2, waiting for transfers between devices, scatter_sum(): lax.psum_scatter(terms, 'heads', scatter_dimension=0, tiled=True)  181 us
    all_to_all x2, waiting for transfers between devices, on_device(): lax.all_to_all(sent.reshape((readers, capacity) + sent.shape[1:]), 'pages...  91.4 us
    all_to_all x2, starting transfers between devices, on_device(): lax.all_to_all(sent.reshape((readers, capacity) + sent.shape[1:]), 'pages...  37.8 us
    all_to_all x1, blocking collectives, gather_rows(): lax.all_to_all(jnp.stack([rows] * lax.axis_size('heads')), 'heads', 0, 0)  26.8 us
    all_to_all x1, blocking collectives, on_device(): lax.all_to_all(asked.reshape(readers, capacity), 'pages', split_axis=0, c...  22.2 us
    all_to_all x1, waiting for transfers between devices, gather_rows(): lax.all_to_all(jnp.stack([rows] * lax.axis_size('heads')), 'heads', 0, 0)  20.7 us
    all_to_all x1, starting transfers between devices, gather_rows(): lax.all_to_all(jnp.stack([rows] * lax.axis_size('heads')), 'heads', 0, 0)  10 us
  transfers between devices with their start and end apart: 5, of which 5 were waited for; matrix products, arithmetic and copies ran while one was open for 5% of the time, Pallas kernels for 0%

profile of v1, /device:TPU:8, one launch (start us, length us, event | category | flops | bytes accessed | tf_op | source)
XLA Modules:
  0.0 446.6 jit_solution(7720646325788906802)
XLA Ops:
  6.5 0.8 copy.31
  7.4 0.2 convert_reduce_fusion.2
  7.7 0.1 all_to_all.18
  7.8 22.2 %all_to_all.29 = s32[64,1,2]{2,1,0:T(1,128)S(1)} all-to-all(s32[64,1,2]{2,1,0:T(1,128)S(1)} %bitcast.71), channel_id=1, replica_groups=mesh['pages'=64,'heads'=8] {'pages'}, dimensions={0} | all-to-all | bytes 1024 | tf_op jit(solution)/shard_map/all_to_all | solution.py:53
  30.1 2.3 stack.4
  32.3 10.0 %all-to-all-start.2 = ((bf16[8,96,1024]{2,1,0:T(8,128)(2,1)}), bf16[8,96,1024]{2,1,0:T(8,128)(2,1)S(1)}, u32[]{:S(2)}, u32[]{:S(2)}) async-start(bf16[8,96,1024]{2,1,0:T(8,128)(2,1)} %stack.4), calls=%async_computation.2 | async-start | bytes 3145728 | tf_op jit(solution)/shard_map/all_to_all | solution.py:19
  42.4 2.9 slice_bitcast_fusion
  45.3 0.5 broadcast.326
  45.8 0.7 reduce.7
  46.5 0.1 reshape.291
  46.7 3.4 gather_fusion
  50.1 2.1 gather_fusion.1
  52.2 4.6 %broadcast_select_fusion = (bf16[128,2,32,128]{3,2,1,0:T(8,128)(2,1)}, bf16[128,2,32,128]{3,2,1,0:T(8,128)(2,1)}) fusion(bf16[128,2,32,128]{3,2,1,0:T(8,128)(2,1)} %gather_fusion.1, pred[128]{0:T(512)(128)(4,1)S(1)} %compare_and_fusion.1, bf16[128,2,32,128]{3,2,1,0:T(8,128)(2,1)} %gather_fusion), kind=kLoop, calls=%fused_computation.16 | loop fusion | flops 2097152 | bytes 8388736 | tf_op jit(solution)/shard_map/jit(_take)/select_n | solution.py:58
  56.9 20.7 %all-to-all-done.2 = bf16[8,96,1024]{2,1,0:T(8,128)(2,1)S(1)} async-done(((bf16[8,96,1024]{2,1,0:T(8,128)(2,1)}), bf16[8,96,1024]{2,1,0:T(8,128)(2,1)S(1)}, u32[]{:S(2)}, u32[]{:S(2)}) %all-to-all-start.2) | async-done | bytes 1572896 | tf_op jit(solution)/shard_map/all_to_all | solution.py:19
  77.6 11.3 %all-to-all-start.1 = ((bf16[64,2,2,32,128]{4,3,2,1,0:T(8,128)(2,1)}), bf16[64,2,2,32,128]{4,3,2,1,0:T(8,128)(2,1)}, u32[]{:S(2)}, u32[]{:S(2)}) async-start(bf16[64,2,2,32,128]{4,3,2,1,0:T(8,128)(2,1)} %bitcast.58), calls=%async_computation.1 | async-start | bytes 4194304 | tf_op jit(solution)/shard_map/all_to_all | solution.py:62
  89.2 0.3 convert_reduce_fusion.1
  89.6 0.6 fusion.6
  90.1 0.4 fusion.7
  90.6 0.6 copy-done.3
  91.1 2.4 fusion.55
  93.5 45.7 %all-to-all-done.1 = bf16[64,2,2,32,128]{4,3,2,1,0:T(8,128)(2,1)} async-done(((bf16[64,2,2,32,128]{4,3,2,1,0:T(8,128)(2,1)}), bf16[64,2,2,32,128]{4,3,2,1,0:T(8,128)(2,1)}, u32[]{:S(2)}, u32[]{:S(2)}) %all-to-all-start.1) | async-done | bytes 2097184 | tf_op jit(solution)/shard_map/all_to_all | solution.py:62
  139.2 0.2 copy.33
  139.5 2.3 gather_fusion.2
  141.8 0.2 broadcast_select_fusion.3
  142.0 0.1 fusion.54
  142.1 0.6 fusion.21
  142.7 0.2 copy.36
  143.1 2.8 convolution_convert_fusion.1
  146.0 90.2 %reduce-scatter.3.cloned.1.call-done = bf16[96,1024]{1,0:T(8,128)(2,1)} async-done(((bf16[768,1024]{1,0:T(8,128)(2,1)}), bf16[96,1024]{1,0:T(8,128)(2,1)}) %reduce-scatter.3.cloned.1.call-update) | async-done | bytes 196624 | tf_op jit(solution)/shard_map/reduce_scatter | solution.py:24
  236.2 1.0 add_convert_fusion.1
  237.2 0.2 stack.5
  237.4 26.8 %all_to_all.30 = bf16[8,96,1024]{2,1,0:T(8,128)(2,1)S(1)} all-to-all(bf16[8,96,1024]{2,1,0:T(8,128)(2,1)S(1)} %stack.5), channel_id=1, replica_groups=mesh['pages'=64,'heads'=8] {'heads'}, dimensions={0} | all-to-all | bytes 3145728 | tf_op jit(solution)/shard_map/all_to_all | solution.py:19
  264.2 26.5 %all-to-all-start.3 = ((bf16[64,2,2,32,128]{4,3,2,1,0:T(8,128)(2,1)}), bf16[64,2,2,32,128]{4,3,2,1,0:T(8,128)(2,1)}, u32[]{:S(2)}, u32[]{:S(2)}) async-start(bf16[64,2,2,32,128]{4,3,2,1,0:T(8,128)(2,1)} %bitcast.57), calls=%async_computation.4 | async-start | bytes 4194304 | tf_op jit(solution)/shard_map/all_to_all | solution.py:62
  290.7 0.2 reduce-scatter.5.cloned.1.call-start
  290.9 0.3 convert_reduce_fusion
  291.2 0.6 fusion.4
  291.8 0.4 fusion.5
  292.3 0.6 copy-done.4
  292.8 2.4 fusion.56
  295.2 45.7 %all-to-all-done.3 = bf16[64,2,2,32,128]{4,3,2,1,0:T(8,128)(2,1)} async-done(((bf16[64,2,2,32,128]{4,3,2,1,0:T(8,128)(2,1)}), bf16[64,2,2,32,128]{4,3,2,1,0:T(8,128)(2,1)}, u32[]{:S(2)}, u32[]{:S(2)}) %all-to-all-start.3) | async-done | bytes 2097184 | tf_op jit(solution)/shard_map/all_to_all | solution.py:62
  341.0 0.2 copy.37
  341.2 2.3 gather_fusion.3
  343.6 0.2 broadcast_select_fusion.2
  343.9 0.6 fusion.20
  344.5 0.2 copy.40
  344.9 2.8 convolution_convert_fusion
  347.6 90.4 %reduce-scatter.5.cloned.1.call-done = bf16[96,1024]{1,0:T(8,128)(2,1)} async-done(((bf16[768,1024]{1,0:T(8,128)(2,1)}), bf16[96,1024]{1,0:T(8,128)(2,1)}) %reduce-scatter.5.cloned.1.call-update) | async-done | bytes 196624 | tf_op jit(solution)/shard_map/reduce_scatter | solution.py:24
  438.1 1.7 add_convert_fusion
  (43 shorter events, 1.2 us)
Async XLA Ops:
  32.3 45.3 %all-to-all-start.2 = ((bf16[8,96,1024]{2,1,0:T(8,128)(2,1)}), bf16[8,96,1024]{2,1,0:T(8,128)(2,1)S(1)}, u32[]{:S(2)}, u32[]{:S(2)}) async-start(bf16[8,96,1024]{2,1,0:T(8,128)(2,1)} %stack.4), calls=%async_computation.2 | async-start | bytes 3145728 | tf_op jit(solution)/shard_map/all_to_all | solution.py:19
  77.6 11.4 %copy-start.2 = (s32[16]{0:T(128)S(1)}, s32[16]{0:T(128)}, u32[]{:S(2)}) copy-start(s32[16]{0:T(128)} %param.15) | copy-start | bytes 196
  77.6 61.6 %all-to-all-start.1 = ((bf16[64,2,2,32,128]{4,3,2,1,0:T(8,128)(2,1)}), bf16[64,2,2,32,128]{4,3,2,1,0:T(8,128)(2,1)}, u32[]{:S(2)}, u32[]{:S(2)}) async-start(bf16[64,2,2,32,128]{4,3,2,1,0:T(8,128)(2,1)} %bitcast.58), calls=%async_computation.1 | async-start | bytes 4194304 | tf_op jit(solution)/shard_map/all_to_all | solution.py:62
  88.9 147.3 %reduce-scatter.3.cloned.1.call-start = ((), (), s32[]{:S(2)}) async-start(), calls=%async_computation.7 | async-start | bytes 1769472 | tf_op jit(solution)/shard_map/reduce_scatter | solution.py:24
  89.5 1.6 copy-start.3
  142.1 1.0 copy-start.1
  143.1 93.1 %copy-start = (bf16[96,1024]{1,0:T(8,128)(2,1)S(1)}, bf16[96,1024]{1,0:T(8,128)(2,1)}, u32[]{:S(2)}) copy-start(bf16[96,1024]{1,0:T(8,128)(2,1)} %param.10) | copy-start | bytes 589828
  264.2 76.8 %all-to-all-start.3 = ((bf16[64,2,2,32,128]{4,3,2,1,0:T(8,128)(2,1)}), bf16[64,2,2,32,128]{4,3,2,1,0:T(8,128)(2,1)}, u32[]{:S(2)}, u32[]{:S(2)}) async-start(bf16[64,2,2,32,128]{4,3,2,1,0:T(8,128)(2,1)} %bitcast.57), calls=%async_computation.4 | async-start | bytes 4194304 | tf_op jit(solution)/shard_map/all_to_all | solution.py:62
  290.7 147.4 %reduce-scatter.5.cloned.1.call-start = ((), (), s32[]{:S(2)}) async-start(), calls=%async_computation.8 | async-start | bytes 1769472 | tf_op jit(solution)/shard_map/reduce_scatter | solution.py:24
  291.2 1.6 copy-start.4
Sparse Core Ops, SparseCore 0:
  146.1 90.0 reduce-scatter.2
  347.8 90.2 reduce-scatter.4
